TPU v7x, 32 devices: a whole 2x2x4 slice. The times are simulated.
32 devices in a mesh: depth: 8 (over z, y), lat: 4 (over x, core).
Axes of the slice: x: 2, y: 2, z: 4, core: 2. Of those that a mesh axis runs over, the one named last changes fastest.
Arguments:
- incident: float32 [8, 2, 2, 128, 128], P('depth', None, None, 'lat'), may hold values from -6 to 6
- contrast: float32 [8, 128, 128], P('depth', 'lat'), may hold values from -0.8 to 0.8
- kernel: bfloat16 [8, 8, 2, 256, 256], P('depth', None, None, 'lat'), may hold values from -6 to 6
Outputs:
- total_field: float32 [8, 2, 2, 128, 128], P('depth', None, None, 'lat')
All inputs are finite; a program needn't handle non-finite values.
Results may differ from a plain program's by a relative error of at most 0.017.
Values may be sent and summed in bfloat16 or wider, within the bound.
A program may use at most 64 MiB of HBM per device.

v0:
```python
import math

import jax
import jax.numpy as jnp
from jax import lax
from jax.sharding import PartitionSpec as P

L = 128
ITERS = 3


def wave_tables(count_in, count_out, period):
    indices = (
        jnp.arange(count_in, dtype=jnp.int32)[:, None]
        * jnp.arange(count_out, dtype=jnp.int32)[None, :]
        % period
    )
    angles = indices.astype(jnp.float32) * (2.0 * math.pi / period)
    return (jnp.cos(angles).astype(jnp.bfloat16), jnp.sin(angles).astype(jnp.bfloat16))


def last_dot(left, right):
    return jnp.einsum("...a,ab->...b", left, right, preferred_element_type=jnp.float32)


def middle_dot(left, right):
    return jnp.einsum("...ak,ab->...kb", left, right, preferred_element_type=jnp.float32)


def forward_pass(values, cosine, sine_table, product):
    real_part = values[..., 0, :, :]
    imag_part = values[..., 1, :, :]
    out_real = product(real_part, cosine) + product(imag_part, sine_table)
    out_imag = product(imag_part, cosine) - product(real_part, sine_table)
    return jnp.stack([out_real, out_imag], axis=-3)


def inverse_pass(values, cosine, sine_table, product):
    real_part = values[..., 0, :, :]
    imag_part = values[..., 1, :, :]
    out_real = product(real_part, cosine) - product(imag_part, sine_table)
    out_imag = product(real_part, sine_table) + product(imag_part, cosine)
    return jnp.stack([out_real, out_imag], axis=-3)


def couple_grid(kern_rows, spectra):
    form = "lwkm,wskm->lskm"
    kern_real = kern_rows[:, :, 0]
    kern_imag = kern_rows[:, :, 1]
    spec_real = spectra[:, :, 0]
    spec_imag = spectra[:, :, 1]
    out_real = jnp.einsum(
        form, kern_real, spec_real, preferred_element_type=jnp.float32
    ) - jnp.einsum(form, kern_imag, spec_imag, preferred_element_type=jnp.float32)
    out_imag = jnp.einsum(
        form, kern_real, spec_imag, preferred_element_type=jnp.float32
    ) + jnp.einsum(form, kern_imag, spec_real, preferred_element_type=jnp.float32)
    return jnp.stack([out_real, out_imag], axis=2)


def local(incident, contrast, kernel):
    period = 2 * L
    forward_cos, forward_sin = wave_tables(L, period, period)
    inverse_cos, inverse_sin = wave_tables(period, L, period)
    fields = incident
    for iteration in range(ITERS):
        sources = (contrast[:, None, None] * fields).astype(jnp.bfloat16)
        along_y = forward_pass(sources, forward_cos, forward_sin, last_dot).astype(jnp.bfloat16)
        spectra = forward_pass(
            lax.all_to_all(along_y, "lat", split_axis=4, concat_axis=3, tiled=True),
            forward_cos,
            forward_sin,
            middle_dot,
        ).astype(jnp.bfloat16)
        summed = couple_grid(kernel, lax.all_gather(spectra, "depth", axis=0, tiled=True))
        scattered = summed.astype(jnp.bfloat16)
        along_x = inverse_pass(scattered, inverse_cos, inverse_sin, last_dot).astype(jnp.bfloat16)
        returned = inverse_pass(
            lax.all_to_all(along_x, "lat", split_axis=4, concat_axis=3, tiled=True),
            inverse_cos,
            inverse_sin,
            middle_dot,
        )
        fields = incident + returned / float(period * period)
    return fields


def solution(mesh):
    in_specs = (
        P("depth", None, None, "lat", None),
        P("depth", "lat", None),
        P("depth", None, None, "lat", None),
    )
    out_specs = P("depth", None, None, "lat", None)
    return jax.shard_map(local, mesh=mesh, in_specs=in_specs, out_specs=out_specs, check_vma=False)
```

profile of v0, /device:TPU:0, one launch (start us, length us, event | category | flops | bytes accessed | tf_op | source)
XLA Modules:
  0.0 215.3 jit_solution(13810164033015086355)
XLA Ops:
  6.5 0.8 multiply_convert_fusion
  10.4 8.2 %all_to_all.108 = bf16[4,2,4096]{2,1,0:T(2,128)(2,1)S(1)} all-to-all(bf16[4,2,4096]{2,1,0:T(2,128)(2,1)S(1)} %reshape.919), channel_id=1, replica_groups=mesh['depth'=8,'lat'=4] {'lat'}, dimensions={0} | all-to-all | bytes 131072 | tf_op jit(solution)/shard_map/all_to_all | solution.py:70
  20.1 0.6 fusion.10
  20.8 0.6 fusion.11
  21.5 0.7 copy.40
  22.3 40.6 %all-gather.4.cloned.1.call-done = bf16[8,2,2,64,256]{4,3,2,1,0:T(8,128)(2,1)} async-done(((bf16[1,2,2,64,256]{4,3,2,1,0:T(8,128)(2,1)}), bf16[8,2,2,64,256]{4,3,2,1,0:T(8,128)(2,1)}) %all-gather.4.cloned.1.call-update) | async-done | bytes 1048592 | tf_op jit(solution)/shard_map/all_gather | solution.py:75
  62.9 1.6 fusion.43
  67.4 6.7 %all_to_all.109 = bf16[4,2,4096]{2,1,0:T(2,128)(2,1)S(1)} all-to-all(bf16[4,2,4096]{2,1,0:T(2,128)(2,1)S(1)} %reshape.921), channel_id=1, replica_groups=mesh['depth'=8,'lat'=4] {'lat'}, dimensions={0} | all-to-all | bytes 131072 | tf_op jit(solution)/shard_map/all_to_all | solution.py:79
  80.2 6.5 %all_to_all.110 = bf16[4,2,4096]{2,1,0:T(2,128)(2,1)S(1)} all-to-all(bf16[4,2,4096]{2,1,0:T(2,128)(2,1)S(1)} %reshape.923), channel_id=1, replica_groups=mesh['depth'=8,'lat'=4] {'lat'}, dimensions={0} | all-to-all | bytes 131072 | tf_op jit(solution)/shard_map/all_to_all | solution.py:70
  88.3 0.6 fusion.8
  89.0 0.6 fusion.9
  89.6 0.7 copy.49
  90.4 38.2 %all-gather.6.cloned.1.call-done = bf16[8,2,2,64,256]{4,3,2,1,0:T(8,128)(2,1)} async-done(((bf16[1,2,2,64,256]{4,3,2,1,0:T(8,128)(2,1)}), bf16[8,2,2,64,256]{4,3,2,1,0:T(8,128)(2,1)}) %all-gather.6.cloned.1.call-update) | async-done | bytes 1048592 | tf_op jit(solution)/shard_map/all_gather | solution.py:75
  128.6 1.6 fusion.47
  132.1 0.6 fusion.29
  133.1 6.7 %all_to_all.111 = bf16[4,2,4096]{2,1,0:T(2,128)(2,1)S(1)} all-to-all(bf16[4,2,4096]{2,1,0:T(2,128)(2,1)S(1)} %reshape.925), channel_id=1, replica_groups=mesh['depth'=8,'lat'=4] {'lat'}, dimensions={0} | all-to-all | bytes 131072 | tf_op jit(solution)/shard_map/all_to_all | solution.py:79
  145.6 6.5 %all_to_all.112 = bf16[4,2,4096]{2,1,0:T(2,128)(2,1)S(1)} all-to-all(bf16[4,2,4096]{2,1,0:T(2,128)(2,1)S(1)} %reshape.927), channel_id=1, replica_groups=mesh['depth'=8,'lat'=4] {'lat'}, dimensions={0} | all-to-all | bytes 131072 | tf_op jit(solution)/shard_map/all_to_all | solution.py:70
  153.8 0.6 fusion.6
  154.4 0.6 fusion.7
  155.1 0.7 copy.58
  155.7 38.3 %all-gather.8.cloned.1.call-done = bf16[8,2,2,64,256]{4,3,2,1,0:T(8,128)(2,1)} async-done(((bf16[1,2,2,64,256]{4,3,2,1,0:T(8,128)(2,1)}), bf16[8,2,2,64,256]{4,3,2,1,0:T(8,128)(2,1)}) %all-gather.8.cloned.1.call-update) | async-done | bytes 1048592 | tf_op jit(solution)/shard_map/all_gather | solution.py:75
  194.0 1.6 fusion.51
  198.5 6.7 %all_to_all.113 = bf16[4,2,4096]{2,1,0:T(2,128)(2,1)S(1)} all-to-all(bf16[4,2,4096]{2,1,0:T(2,128)(2,1)S(1)} %reshape.929), channel_id=1, replica_groups=mesh['depth'=8,'lat'=4] {'lat'}, dimensions={0} | all-to-all | bytes 131072 | tf_op jit(solution)/shard_map/all_to_all | solution.py:79
  208.1 0.6 copy.63
  (101 shorter events, 30.7 us)
Async XLA Ops:
  6.5 56.4 %all-gather.4.cloned.1.call-start = ((), (), s32[]{:S(2)}) async-start(), calls=%async_computation.6 | async-start | bytes 1179648 | tf_op jit(solution)/shard_map/all_gather | solution.py:75
  20.8 1.4 copy-start.1
  22.1 106.4 %all-gather.6.cloned.1.call-start = ((), (), s32[]{:S(2)}) async-start(), calls=%async_computation.7 | async-start | bytes 1179648 | tf_op jit(solution)/shard_map/all_gather | solution.py:75
  76.4 0.9 copy-start
  76.4 0.9 copy-start.2
  90.3 103.7 %all-gather.8.cloned.1.call-start = ((), (), s32[]{:S(2)}) async-start(), calls=%async_computation.8 | async-start | bytes 1179648 | tf_op jit(solution)/shard_map/all_gather | solution.py:75
Sparse Core Ops, SparseCore 0:
  22.3 40.5 all-gather.3
  90.4 38.0 all-gather.5
  155.9 38.0 all-gather.7
where the time goes:
time: 216 us; the launch traced here: 215 us
  waiting for transfers between devices  117 us (54%)
  blocking collectives  41.1 us (19%)
  matrix products  30 us (14%)
  between operations  13.6 us (6%)
  local copies, waits for them, and re-layouts  7.3 us (3%)
  other arithmetic  6.13 us (3%)
    all_gather x3, waiting for transfers between devices, local(): lax.all_gather(spectra, 'depth', axis=0, tiled=True)  117 us
    all_to_all x3, blocking collectives, local(): lax.all_to_all(along_y, 'lat', split_axis=4, concat_axis=3, tiled=True)  21.1 us
    all_to_all x3, blocking collectives, local(): lax.all_to_all(along_x, 'lat', split_axis=4, concat_axis=3, tiled=True)  20 us
    dot_general x24, matrix products, middle_dot(): jnp.einsum('...ak,ab->...kb', left, right, preferred_element_type=jnp.flo...  15 us
    dot_general x24, matrix products, last_dot(): jnp.einsum('...a,ab->...b', left, right, preferred_element_type=jnp.float32)  15 us
    dot_general x3, other arithmetic, couple_grid(): jnp.einsum(form, kern_imag, spec_real, preferred_element_type=jnp.float32)  4.89 us
  transfers between devices with their start and end apart: 3, of which 3 were waited for; matrix products, arithmetic and copies ran while one was open for 0% of the time, Pallas kernels for 0%

commit v1 on v0

--- a/solution.py
+++ b/solution.py
@@ -1,12 +1,17 @@
+import functools
 import math
 
 import jax
 import jax.numpy as jnp
+import numpy as np
 from jax import lax
+from jax.experimental import pallas as pl
+from jax.experimental.pallas import tpu as pltpu
 from jax.sharding import PartitionSpec as P
 
 L = 128
 ITERS = 3
+MESH = pl.DeviceIdType.MESH
 
 
 def wave_tables(count_in, count_out, period):
@@ -85,6 +90,220 @@
     return fields
 
 
+def dft(rows, columns, period):
+    angles = (np.outer(np.arange(rows), np.arange(columns)) % period) * (2.0 * math.pi / period)
+    return np.cos(angles), np.sin(angles)
+
+
+def tables(length, lats):
+    period = 2 * length
+    part = length // lats
+    cos_f, sin_f = dft(length, period, period)
+    cos_i, sin_i = dft(period, length, period)
+    forward_y = np.concatenate([cos_f.T, sin_f.T], axis=1)
+    inverse_y = np.concatenate([cos_i, sin_i], axis=1)
+    real_rows = np.concatenate([cos_f, -sin_f], axis=1).reshape(lats, part, 2 * period)
+    imag_rows = np.concatenate([sin_f, cos_f], axis=1).reshape(lats, part, 2 * period)
+    forward_x = np.stack([real_rows, imag_rows], axis=1).reshape(2 * length, 2 * period)
+    to_real = np.concatenate([cos_i, -sin_i], axis=0).reshape(2 * period, lats, part)
+    to_imag = np.concatenate([sin_i, cos_i], axis=0).reshape(2 * period, lats, part)
+    inverse_x = np.stack([to_real, to_imag], axis=2).reshape(2 * period, 2 * length)
+    return tuple(jnp.asarray(t, jnp.bfloat16) for t in (forward_y, forward_x, inverse_x, inverse_y))
+
+
+def born_kernel(
+    depths, lats,
+    incident, contrast, green, forward_y, forward_x, inverse_x, inverse_y, out,
+    slabs, out_a, in_a, out_b, in_b, spectra, scattered,
+    slab_send, slab_recv, send_a, recv_a, send_b, recv_b,
+):
+    depth = lax.axis_index("depth")
+    lat = lax.axis_index("lat")
+    devices = depths * lats
+    me = depth * lats + lat
+    rows = out_a.shape[1]
+    sources_count, _, part, length = incident.shape[1:]
+    lanes = 2 * part
+    period = inverse_y.shape[0]
+
+    def peer(k):
+        number = lax.rem(me + k, devices)
+        return number // lats, lax.rem(number, lats)
+
+    barrier = pltpu.get_barrier_semaphore()
+
+    def greet(k, carry):
+        pl.semaphore_signal(barrier, inc=1, device_id=peer(k), device_id_type=MESH)
+        return carry
+
+    lax.fori_loop(1, devices, greet, 0)
+
+    own = pltpu.make_async_copy(
+        green.at[0, :, :, pl.ds(pl.multiple_of(depth * rows, rows), rows)],
+        slabs.at[depth],
+        slab_recv.at[depth],
+    )
+    own.start()
+
+    def halves(field):
+        return field.reshape(sources_count, 2, part, length)
+
+    def spread_along_y(field):
+        driven = contrast[0][None, None] * halves(field)
+        turned = jnp.concatenate([driven[:, 1:2], -driven[:, 0:1]], axis=1)
+        flat = (sources_count * 2 * part, length)
+        both = jnp.concatenate([driven.reshape(flat), turned.reshape(flat)], axis=1).astype(jnp.bfloat16)
+        along_y = lax.dot_general(
+            forward_y[...], both, (((1,), (1,)), ((), ())), preferred_element_type=jnp.float32
+        )
+        out_a[...] = along_y.reshape(out_a.shape).astype(jnp.bfloat16)
+
+    def exchange_a():
+        def send(k, carry):
+            d, l = peer(k)
+            pltpu.make_async_remote_copy(
+                out_a.at[l * depths + d], in_a.at[depth, lat], send_a, recv_a,
+                device_id=(d, l), device_id_type=MESH,
+            ).start()
+            return carry
+
+        pltpu.make_async_copy(out_a.at[lat * depths + depth], in_a.at[depth, lat], recv_a).start()
+        lax.fori_loop(1, devices, send, 0)
+
+    def exchange_b():
+        def send(k, carry):
+            d, l = peer(k)
+            pltpu.make_async_remote_copy(
+                out_b.at[d, l], in_b.at[lat * depths + depth], send_b, recv_b,
+                device_id=(d, l), device_id_type=MESH,
+            ).start()
+            return carry
+
+        pltpu.make_async_copy(out_b.at[depth, lat], in_b.at[lat * depths + depth], recv_b).start()
+        lax.fori_loop(1, devices, send, 0)
+
+    def slab_copy(k):
+        d = lax.rem(depth + k, depths)
+        return pltpu.make_async_remote_copy(
+            green.at[0, :, :, pl.ds(pl.multiple_of(d * rows, rows), rows)],
+            slabs.at[depth], slab_send.at[d], slab_recv.at[depth],
+            device_id=(d, lat), device_id_type=MESH,
+        )
+
+    field = incident[...].reshape(sources_count * 2 * part, length)
+    for iteration in range(ITERS):
+        spread_along_y(field)
+        if iteration == 0:
+            pl.semaphore_wait(barrier, devices - 1)
+        exchange_a()
+        if iteration == 0:
+            def deal(k, carry):
+                slab_copy(k).start()
+                return carry
+
+            lax.fori_loop(1, depths, deal, 0)
+        pltpu.make_async_copy(in_a, in_a, recv_a).wait()
+        blocks = [
+            in_a[:, l].astype(jnp.float32).reshape(depths * rows, sources_count * lanes)
+            for l in range(lats)
+        ]
+        for s in range(sources_count):
+            half = jnp.concatenate(
+                [b[:, s * lanes:(s + 1) * lanes] for b in blocks], axis=1
+            ).astype(jnp.bfloat16)
+            spectra[s] = jnp.dot(
+                half, forward_x[...], preferred_element_type=jnp.float32
+            ).reshape(depths, rows, 2 * period)
+
+        def couple(k, carry):
+            z = lax.rem(depth + k, depths)
+            if iteration == 0:
+                pltpu.make_async_copy(slabs.at[z], slabs.at[z], slab_recv.at[z]).wait()
+            reals = [jnp.zeros((rows, period), jnp.float32) for _ in range(sources_count)]
+            imags = [jnp.zeros((rows, period), jnp.float32) for _ in range(sources_count)]
+            for w in range(depths):
+                kern_real = slabs[z, w, 0].astype(jnp.float32)
+                kern_imag = slabs[z, w, 1].astype(jnp.float32)
+                for s in range(sources_count):
+                    spec_real = spectra[s, w, :, :period]
+                    spec_imag = spectra[s, w, :, period:]
+                    reals[s] += kern_real * spec_real - kern_imag * spec_imag
+                    imags[s] += kern_real * spec_imag + kern_imag * spec_real
+            for s in range(sources_count):
+                scattered[s, z, :, :period] = reals[s]
+                scattered[s, z, :, period:] = imags[s]
+            return carry
+
+        lax.fori_loop(0, depths, couple, 0)
+        returned = [
+            jnp.dot(
+                scattered[s].reshape(depths * rows, 2 * period).astype(jnp.bfloat16),
+                inverse_x[...],
+                preferred_element_type=jnp.float32,
+            )
+            for s in range(sources_count)
+        ]
+        pltpu.make_async_copy(out_a.at[1:], out_a.at[1:], send_a).wait()
+        for l in range(lats):
+            out_b[:, l] = jnp.concatenate(
+                [r[:, l * lanes:(l + 1) * lanes] for r in returned], axis=1
+            ).reshape(depths, rows, sources_count * lanes).astype(jnp.bfloat16)
+        exchange_b()
+        pltpu.make_async_copy(in_b, in_b, recv_b).wait()
+        along_x = in_b[...].astype(jnp.float32).reshape(period, sources_count * lanes).astype(jnp.bfloat16)
+        turned = lax.dot_general(
+            along_x, inverse_y[...], (((0,), (0,)), ((), ())), preferred_element_type=jnp.float32
+        )
+        cosine = halves(turned[:, :length])
+        sine = halves(turned[:, length:])
+        sums = jnp.concatenate(
+            [cosine[:, 0:1] - sine[:, 1:2], cosine[:, 1:2] + sine[:, 0:1]], axis=1
+        )
+        field = (incident[0] + sums * (1.0 / float(period * period))).reshape(field.shape)
+        slots = out_b.reshape(devices, rows, sources_count * lanes)
+        pltpu.make_async_copy(slots.at[1:], slots.at[1:], send_b).wait()
+    out[...] = field.reshape(out.shape)
+
+    def sent(k, carry):
+        slab_copy(k).wait_send()
+        return carry
+
+    lax.fori_loop(1, depths, sent, 0)
+
+
+def born(depths, lats, incident, contrast, kernel):
+    sources_count, part, length = incident.shape[1], incident.shape[3], incident.shape[4]
+    devices = depths * lats
+    period = 2 * length
+    rows = period // devices
+    lanes = sources_count * 2 * part
+    vmem = pl.BlockSpec(memory_space=pltpu.VMEM)
+    block = jnp.bfloat16
+    return pl.pallas_call(
+        functools.partial(born_kernel, depths, lats),
+        out_shape=jax.ShapeDtypeStruct(incident.shape, jnp.float32),
+        in_specs=[vmem, vmem, pl.BlockSpec(memory_space=pl.ANY)] + [vmem] * 4,
+        out_specs=vmem,
+        scratch_shapes=[
+            pltpu.VMEM((depths, depths, 2, rows, period), block),
+            pltpu.VMEM((devices, rows, lanes), block),
+            pltpu.VMEM((depths, lats, rows, lanes), block),
+            pltpu.VMEM((depths, lats, rows, lanes), block),
+            pltpu.VMEM((devices, rows, lanes), block),
+            pltpu.VMEM((sources_count, depths, rows, 2 * period), jnp.float32),
+            pltpu.VMEM((sources_count, depths, rows, 2 * period), jnp.float32),
+            pltpu.SemaphoreType.DMA((depths,)),
+            pltpu.SemaphoreType.DMA((depths,)),
+            pltpu.SemaphoreType.DMA,
+            pltpu.SemaphoreType.DMA,
+            pltpu.SemaphoreType.DMA,
+            pltpu.SemaphoreType.DMA,
+        ],
+        compiler_params=pltpu.CompilerParams(collective_id=0, has_side_effects=True),
+        name="born",
+    )(incident, contrast, kernel, *tables(length, lats))
+
+
 def solution(mesh):
     in_specs = (
         P("depth", None, None, "lat", None),
@@ -92,4 +311,11 @@
         P("depth", None, None, "lat", None),
     )
     out_specs = P("depth", None, None, "lat", None)
-    return jax.shard_map(local, mesh=mesh, in_specs=in_specs, out_specs=out_specs, check_vma=False)
+    depths, lats = mesh.shape["depth"], mesh.shape["lat"]
+
+    def run(incident, contrast, kernel):
+        if (2 * incident.shape[4]) % (8 * depths * lats) == 0:
+            return born(depths, lats, incident, contrast, kernel)
+        return local(incident, contrast, kernel)
+
+    return jax.shard_map(run, mesh=mesh, in_specs=in_specs, out_specs=out_specs, check_vma=False)

time: 216 us -> 53.1 us (0.25)
  waiting for transfers between devices: 117 us -> 0 us
  Pallas kernels: 0 us -> 51.4 us
  blocking collectives: 41.1 us -> 0 us
  matrix products: 30 us -> 0 us
  between operations: 13.6 us -> 0.01 us
  other arithmetic: 6.13 us -> 0 us
  local copies, waits for them, and re-layouts: 7.3 us -> 1.47 us
    all_gather x3 -> x0, waiting for transfers between devices: 117 us -> none  [local(): lax.all_gather(spectra, 'depth', axis=0, tiled=True)]
    pallas_call x0 -> x1, Pallas kernels: none -> 51.4 us  [born(): pl.pallas_call(functools.partial(born_kernel, depths, lats), out_shape=ja...]
    all_to_all x6 -> x0, blocking collectives: 41.1 us -> none  [the longest x3 21.1 us: local(): lax.all_to_all(along_y, 'lat', split_axis=4, concat_axis=3, tiled=True)]
    dot_general x48 -> x0, matrix products: 30 us -> none  [the longest x24 15 us: middle_dot(): jnp.einsum('...ak,ab->...kb', left, right, preferred_element_type=jnp.flo...]
    dot_general x3 -> x0, other arithmetic: 4.89 us -> none  [couple_grid(): jnp.einsum(form, kern_imag, spec_real, preferred_element_type=jnp.float32)]
    another operation x9 -> x0, local copies, waits for them, and re-layouts: 2.84 us -> none  [the longest x6 2.46 us: forward_pass(): return jnp.stack([out_real, out_imag], axis=-3)]
  transfers between devices with their start and end apart: 3 -> 0, of which waited for: 3 -> 0; matrix products, arithmetic and copies ran while one was open for 0% -> 0% of each run, Pallas kernels for 0% -> 0%
where the time goes in v1:
time: 53.1 us; the launch traced here: 52.9 us
  Pallas kernels  51.4 us (97%)
  local copies, waits for them, and re-layouts  1.47 us (3%)
    pallas_call x1, Pallas kernels, born(): pl.pallas_call(functools.partial(born_kernel, depths, lats), out_shape=ja...  51.4 us
    unnamed x1, local copies, waits for them, and re-layouts  1.47 us

profile of v1, /device:TPU:0, one launch (start us, length us, event | category | flops | bytes accessed | tf_op | source)
XLA Modules:
  0.0 52.9 jit_solution(697835421124777125)
XLA Ops:
  0.0 51.4 %born.1 = f32[1,2,2,32,128]{4,3,2,1,0:T(8,128)} custom-call(f32[1,2,2,32,128]{4,3,2,1,0:T(8,128)} %incident.1, f32[1,32,128]{2,1,0:T(8,128)} %contrast.1, bf16[1,8,2,64,256]{4,3,2,1,0:T(8,128)(2,1)} %green.1, bf16[256,256]{1,0:T(8,128)(2,1)} %constant.6.clone.forward_y.inverse_y, bf16[256,512]{1,0:T(8,128)(2,1)} %constant.7.clone.forward_x, ...), custom_call_target="tpu_custom_call" | custom-call | tf_op jit(solution)/shard_map/born/pallas_call | solution.py:282
  51.4 1.5 %copy.9 = f32[1,2,2,32,128]{4,3,2,1,0:T(8,128)} copy(f32[1,2,2,32,128]{4,3,2,1,0:T(8,128)} %born.1) | data formatting | bytes 131072

commit v2 on v1

v2 whole, which is shorter than its diff:
```python
import functools
import math

import jax
import jax.numpy as jnp
import numpy as np
from jax import lax
from jax.experimental import pallas as pl
from jax.experimental.pallas import tpu as pltpu
from jax.sharding import PartitionSpec as P

ITERS = 3
GROUP = 4
MESH = pl.DeviceIdType.MESH


def dft(rows, columns, period):
    angles = (np.outer(np.arange(rows), np.arange(columns)) % period) * (2.0 * math.pi / period)
    return np.cos(angles), np.sin(angles)


def tables(length, lats):
    period = 2 * length
    part = length // lats
    cos_f, sin_f = dft(length, period, period)
    cos_i, sin_i = dft(period, length, period)
    forward_y = np.concatenate([cos_f.T, sin_f.T], axis=1)
    inverse_y = np.concatenate([cos_i, sin_i], axis=1)
    real_rows = np.concatenate([cos_f, -sin_f], axis=1).reshape(lats, part, 2 * period)
    imag_rows = np.concatenate([sin_f, cos_f], axis=1).reshape(lats, part, 2 * period)
    forward_x = np.stack([real_rows, imag_rows], axis=1).reshape(2 * length, 2 * period)
    to_real = np.concatenate([cos_i, -sin_i], axis=0).reshape(2 * period, lats, part)
    to_imag = np.concatenate([sin_i, cos_i], axis=0).reshape(2 * period, lats, part)
    inverse_x = np.stack([to_real, to_imag], axis=2).reshape(2 * period, 2 * length)
    return tuple(jnp.asarray(t, jnp.bfloat16) for t in (forward_y, forward_x, inverse_x, inverse_y))


def born_kernel(
    depths, lats, group,
    incident, contrast, green, forward_y, forward_x, inverse_x, inverse_y, out,
    slabs, out_a, in_a, out_b, in_b, spectra, scattered,
    slab_send, slab_recv, send_a, recv_a, send_b, recv_b,
):
    depth = lax.axis_index("depth")
    lat = lax.axis_index("lat")
    devices = depths * lats
    me = depth * lats + lat
    place = lax.rem(depth, group)
    first = depth - place
    rows = out_a.shape[1]
    sources_count, _, part, length = incident.shape[1:]
    lanes = 2 * part
    period = inverse_y.shape[0]

    def peer(k):
        number = lax.rem(me + k, devices)
        return number // lats, lax.rem(number, lats)

    def member(k):
        number = lax.rem(place * lats + lat + k, group * lats)
        return number // lats, lax.rem(number, lats)

    barrier = pltpu.get_barrier_semaphore()

    def greet(k, carry):
        pl.semaphore_signal(barrier, inc=1, device_id=peer(k), device_id_type=MESH)
        return carry

    lax.fori_loop(1, devices, greet, 0)

    own = pltpu.make_async_copy(
        green.at[0, :, :, pl.ds(pl.multiple_of(place * rows, rows), rows)],
        slabs.at[place],
        slab_recv.at[place],
    )
    own.start()

    def halves(field):
        return field.reshape(sources_count, 2, part, length)

    def spread_along_y(field):
        driven = contrast[0][None, None] * halves(field)
        turned = jnp.concatenate([driven[:, 1:2], -driven[:, 0:1]], axis=1)
        flat = (sources_count * 2 * part, length)
        both = jnp.concatenate([driven.reshape(flat), turned.reshape(flat)], axis=1).astype(jnp.bfloat16)
        along_y = lax.dot_general(
            forward_y[...], both, (((1,), (1,)), ((), ())), preferred_element_type=jnp.float32
        )
        out_a[...] = along_y.reshape(out_a.shape).astype(jnp.bfloat16)

    def exchange_a(slot):
        def send(k, carry):
            d, l = peer(k)
            pltpu.make_async_remote_copy(
                out_a.at[l * group + lax.rem(d, group)], in_a.at[slot, depth, lat], send_a, recv_a.at[slot],
                device_id=(d, l), device_id_type=MESH,
            ).start()
            return carry

        pltpu.make_async_copy(out_a.at[lat * group + place], in_a.at[slot, depth, lat], recv_a.at[slot]).start()
        lax.fori_loop(1, devices, send, 0)

    def exchange_b():
        def send(k, carry):
            d, l = member(k)
            pltpu.make_async_remote_copy(
                out_b.at[d, l], in_b.at[lat * group + place], send_b, recv_b,
                device_id=(first + d, l), device_id_type=MESH,
            ).start()
            return carry

        pltpu.make_async_copy(out_b.at[place, lat], in_b.at[lat * group + place], recv_b).start()
        lax.fori_loop(1, group * lats, send, 0)

    def slab_copy(k):
        d = lax.rem(place + k, group)
        return pltpu.make_async_remote_copy(
            green.at[0, :, :, pl.ds(pl.multiple_of(d * rows, rows), rows)],
            slabs.at[place], slab_send.at[d], slab_recv.at[place],
            device_id=(first + d, lat), device_id_type=MESH,
        )

    field = incident[...].reshape(sources_count * 2 * part, length)
    for iteration in range(ITERS):
        spread_along_y(field)
        if iteration == 0:
            pl.semaphore_wait(barrier, devices - 1)
        slot = iteration % 2
        exchange_a(slot)
        if iteration == 0:
            def deal(k, carry):
                slab_copy(k).start()
                return carry

            lax.fori_loop(1, group, deal, 0)
        pltpu.make_async_copy(in_a.at[slot], in_a.at[slot], recv_a.at[slot]).wait()
        blocks = [
            in_a[slot, :, l].astype(jnp.float32).reshape(depths * rows, sources_count * lanes)
            for l in range(lats)
        ]
        for s in range(sources_count):
            half = jnp.concatenate(
                [b[:, s * lanes:(s + 1) * lanes] for b in blocks], axis=1
            ).astype(jnp.bfloat16)
            spectra[s] = jnp.dot(
                half, forward_x[...], preferred_element_type=jnp.float32
            ).reshape(depths, rows, 2 * period)

        def couple(k, carry):
            z = lax.rem(place + k, group)
            if iteration == 0:
                pltpu.make_async_copy(slabs.at[z], slabs.at[z], slab_recv.at[z]).wait()
            zero = jnp.zeros((rows, period), jnp.float32)

            def add(w, sums):
                kern_real = slabs[z, w, 0].astype(jnp.float32)
                kern_imag = slabs[z, w, 1].astype(jnp.float32)
                new = []
                for s in range(sources_count):
                    spec_real = spectra[s, w, :, :period]
                    spec_imag = spectra[s, w, :, period:]
                    new.append(sums[2 * s] + (kern_real * spec_real - kern_imag * spec_imag))
                    new.append(sums[2 * s + 1] + (kern_real * spec_imag + kern_imag * spec_real))
                return tuple(new)

            sums = lax.fori_loop(0, depths, add, (zero,) * (2 * sources_count), unroll=4)
            for s in range(sources_count):
                scattered[s, z, :, :period] = sums[2 * s]
                scattered[s, z, :, period:] = sums[2 * s + 1]
            return carry

        lax.fori_loop(0, group, couple, 0)
        returned = [
            jnp.dot(
                scattered[s].reshape(group * rows, 2 * period).astype(jnp.bfloat16),
                inverse_x[...],
                preferred_element_type=jnp.float32,
            )
            for s in range(sources_count)
        ]
        flat_a = in_a.at[slot].reshape(devices, rows, sources_count * lanes)
        pltpu.make_async_copy(flat_a.at[1:], flat_a.at[1:], send_a).wait()
        for l in range(lats):
            out_b[:, l] = jnp.concatenate(
                [r[:, l * lanes:(l + 1) * lanes] for r in returned], axis=1
            ).reshape(group, rows, sources_count * lanes).astype(jnp.bfloat16)
        exchange_b()
        pltpu.make_async_copy(in_b, in_b, recv_b).wait()
        along_x = in_b[...].astype(jnp.float32).reshape(period, sources_count * lanes).astype(jnp.bfloat16)
        turned = lax.dot_general(
            along_x, inverse_y[...], (((0,), (0,)), ((), ())), preferred_element_type=jnp.float32
        )
        cosine = halves(turned[:, :length])
        sine = halves(turned[:, length:])
        sums = jnp.concatenate(
            [cosine[:, 0:1] - sine[:, 1:2], cosine[:, 1:2] + sine[:, 0:1]], axis=1
        )
        field = (incident[0] + sums * (1.0 / float(period * period))).reshape(field.shape)
        pltpu.make_async_copy(in_b.at[1:], in_b.at[1:], send_b).wait()
    out[...] = field.reshape(out.shape)

    def sent(k, carry):
        slab_copy(k).wait_send()
        return carry

    lax.fori_loop(1, group, sent, 0)


def born(depths, lats, incident, contrast, kernel):
    sources_count, part, length = incident.shape[1], incident.shape[3], incident.shape[4]
    period = 2 * length
    group = math.gcd(GROUP, depths)
    rows = period // (group * lats)
    lanes = sources_count * 2 * part
    vmem = pl.BlockSpec(memory_space=pltpu.VMEM)
    block = jnp.bfloat16
    return pl.pallas_call(
        functools.partial(born_kernel, depths, lats, group),
        out_shape=jax.ShapeDtypeStruct(incident.shape, jnp.float32),
        in_specs=[vmem, vmem, pl.BlockSpec(memory_space=pl.ANY)] + [vmem] * 4,
        out_specs=vmem,
        scratch_shapes=[
            pltpu.VMEM((group, depths, 2, rows, period), block),
            pltpu.VMEM((group * lats, rows, lanes), block),
            pltpu.VMEM((2, depths, lats, rows, lanes), block),
            pltpu.VMEM((group, lats, rows, lanes), block),
            pltpu.VMEM((group * lats, rows, lanes), block),
            pltpu.VMEM((sources_count, depths, rows, 2 * period), jnp.float32),
            pltpu.VMEM((sources_count, group, rows, 2 * period), jnp.float32),
            pltpu.SemaphoreType.DMA((group,)),
            pltpu.SemaphoreType.DMA((group,)),
            pltpu.SemaphoreType.DMA,
            pltpu.SemaphoreType.DMA((2,)),
            pltpu.SemaphoreType.DMA,
            pltpu.SemaphoreType.DMA,
        ],
        compiler_params=pltpu.CompilerParams(collective_id=0, has_side_effects=True),
        name="born",
    )(incident, contrast, kernel, *tables(length, lats))


def solution(mesh):
    in_specs = (
        P("depth", None, None, "lat", None),
        P("depth", "lat", None),
        P("depth", None, None, "lat", None),
    )
    out_specs = P("depth", None, None, "lat", None)
    run = functools.partial(born, mesh.shape["depth"], mesh.shape["lat"])
    return jax.shard_map(run, mesh=mesh, in_specs=in_specs, out_specs=out_specs, check_vma=False)
```

time: 53.1 us -> 46.5 us (0.88)
  Pallas kernels: 51.4 us -> 44.8 us
    pallas_call x1, Pallas kernels: 51.4 us -> 44.8 us  [born(): pl.pallas_call(functools.partial(born_kernel, depths, lats, group), out_s...]
where the time goes in v2:
time: 46.5 us; the launch traced here: 46.3 us
  Pallas kernels  44.8 us (96%)
  local copies, waits for them, and re-layouts  1.47 us (3%)
    pallas_call x1, Pallas kernels, born(): pl.pallas_call(functools.partial(born_kernel, depths, lats, group), out_s...  44.8 us
    unnamed x1, local copies, waits for them, and re-layouts  1.47 us

profile of v2, /device:TPU:0, one launch (start us, length us, event | category | flops | bytes accessed | tf_op | source)
XLA Modules:
  0.0 46.3 jit_solution(10363819625128959420)
XLA Ops:
  0.0 44.8 %born.1 = f32[1,2,2,32,128]{4,3,2,1,0:T(8,128)} custom-call(f32[1,2,2,32,128]{4,3,2,1,0:T(8,128)} %incident.1, f32[1,32,128]{2,1,0:T(8,128)} %contrast.1, bf16[1,8,2,64,256]{4,3,2,1,0:T(8,128)(2,1)} %green.1, bf16[256,256]{1,0:T(8,128)(2,1)} %constant.6.clone.forward_y.inverse_y, bf16[256,512]{1,0:T(8,128)(2,1)} %constant.7.clone.forward_x, ...), custom_call_target="tpu_custom_call" | custom-call | tf_op jit(solution)/shard_map/born/pallas_call | solution.py:217
  44.8 1.5 %copy.9 = f32[1,2,2,32,128]{4,3,2,1,0:T(8,128)} copy(f32[1,2,2,32,128]{4,3,2,1,0:T(8,128)} %born.1) | data formatting | bytes 131072

commit v3 on v2

v3 whole, which is shorter than its diff:
```python
import functools
import math

import jax
import jax.numpy as jnp
import numpy as np
from jax import lax
from jax.experimental import pallas as pl
from jax.experimental.pallas import tpu as pltpu
from jax.sharding import PartitionSpec as P

ITERS = 3
GROUP = 4
MESH = pl.DeviceIdType.MESH


def dft(rows, columns, period):
    angles = (np.outer(np.arange(rows), np.arange(columns)) % period) * (2.0 * math.pi / period)
    return np.cos(angles), np.sin(angles)


def tables(length, lats):
    period = 2 * length
    part = length // lats
    cos_f, sin_f = dft(length, period, period)
    cos_i, sin_i = dft(period, length, period)
    waves_y = np.concatenate([cos_i, sin_i], axis=1)
    real_rows = np.concatenate([cos_f, -sin_f], axis=1).reshape(lats, part, 2 * period)
    imag_rows = np.concatenate([sin_f, cos_f], axis=1).reshape(lats, part, 2 * period)
    forward_x = np.stack([real_rows, imag_rows], axis=1).reshape(2 * length, 2 * period)
    to_real = np.concatenate([cos_i, -sin_i], axis=0).reshape(2 * period, lats, part)
    to_imag = np.concatenate([sin_i, cos_i], axis=0).reshape(2 * period, lats, part)
    inverse_x = np.stack([to_real, to_imag], axis=2).reshape(2 * period, 2 * length)
    return tuple(jnp.asarray(t, jnp.bfloat16) for t in (waves_y, forward_x, inverse_x))


def born_kernel(
    depths, lats, group,
    incident_hbm, contrast_hbm, green, waves_y_hbm, forward_x_hbm, inverse_x_hbm, out,
    incident, contrast, waves_y, forward_x, inverse_x,
    slabs, out_a, in_a, out_b, in_b, spectra, scattered,
    loads, slab_send, slab_recv, send_a, recv_a, send_b, recv_b,
):
    depth = lax.axis_index("depth")
    lat = lax.axis_index("lat")
    devices = depths * lats
    members = group * lats
    me = depth * lats + lat
    place = lax.rem(depth, group)
    first = depth - place
    half = out_a.shape[2]
    rows = 2 * half
    sources_count, _, part, length = incident.shape[1:]
    lanes = 2 * part
    period = 2 * length

    def peer(k):
        number = lax.rem(me + k, devices)
        return number // lats, lax.rem(number, lats)

    def member(k):
        number = lax.rem(place * lats + lat + k, members)
        return number // lats, lax.rem(number, lats)

    barrier = pltpu.get_barrier_semaphore()

    def greet(k, carry):
        pl.semaphore_signal(barrier, inc=1, device_id=peer(k), device_id_type=MESH)
        return carry

    lax.fori_loop(1, devices, greet, 0)

    pairs = (
        (contrast_hbm, contrast), (incident_hbm, incident), (waves_y_hbm, waves_y),
        (forward_x_hbm, forward_x), (inverse_x_hbm, inverse_x),
    )
    copies = [pltpu.make_async_copy(a, b, loads.at[n]) for n, (a, b) in enumerate(pairs)]
    own = pltpu.make_async_copy(
        green.at[0, :, :, pl.ds(pl.multiple_of(place * rows, rows), rows)],
        slabs.at[place],
        slab_recv.at[place],
    )
    for copy in copies:
        copy.start()
    own.start()

    def spread_along_y(s, field):
        driven = contrast[0][None] * field.reshape(2, part, length)
        turned = jnp.concatenate([driven[1:2], -driven[0:1]], axis=0)
        both = jnp.concatenate(
            [driven.reshape(lanes, length), turned.reshape(lanes, length)], axis=1
        ).astype(jnp.bfloat16)
        along_y = lax.dot_general(
            waves_y[...], both, (((1,), (1,)), ((), ())), preferred_element_type=jnp.float32
        ).reshape(members, 2, half, lanes)
        out_a[s] = jnp.concatenate([along_y[:, 0], along_y[:, 1]], axis=-1).astype(jnp.bfloat16)

    def exchange_a(slot, s):
        def start(d, l):
            pltpu.make_async_remote_copy(
                out_a.at[s, l * group + lax.rem(d, group)], in_a.at[slot, s, depth, lat],
                send_a.at[s], recv_a.at[slot, s],
                device_id=(d, l), device_id_type=MESH,
            ).start()

        def far(k, carry):
            d, l = member(lax.rem(k, members))
            start(lax.rem(first + (k // members + 1) * group, depths) + d, l)
            return carry

        def near(k, carry):
            d, l = member(k)
            start(first + d, l)
            return carry

        lax.fori_loop(0, devices - members, far, 0, unroll=members)
        lax.fori_loop(1, members, near, 0, unroll=True)
        pltpu.make_async_copy(
            out_a.at[s, lat * group + place], in_a.at[slot, s, depth, lat], recv_a.at[slot, s]
        ).start()

    def sent_a(s):
        block = in_a.at[0, s].reshape(devices, half, 2 * lanes).at[1:]
        pltpu.make_async_copy(block, block, send_a.at[s]).wait()

    def exchange_b(s):
        def send(k, carry):
            d, l = member(k)
            pltpu.make_async_remote_copy(
                out_b.at[s, d, l], in_b.at[s, lat * group + place], send_b.at[s], recv_b.at[s],
                device_id=(first + d, l), device_id_type=MESH,
            ).start()
            return carry

        lax.fori_loop(1, members, send, 0, unroll=True)
        pltpu.make_async_copy(
            out_b.at[s, place, lat], in_b.at[s, lat * group + place], recv_b.at[s]
        ).start()

    def sent_b(s):
        block = in_b.at[s, 1:]
        pltpu.make_async_copy(block, block, send_b.at[s]).wait()

    def slab_copy(k):
        d = lax.rem(place + k, group)
        return pltpu.make_async_remote_copy(
            green.at[0, :, :, pl.ds(pl.multiple_of(d * rows, rows), rows)],
            slabs.at[place], slab_send.at[d], slab_recv.at[place],
            device_id=(first + d, lat), device_id_type=MESH,
        )

    def couple(s, wait_slabs):
        zero = jnp.zeros((rows, period), jnp.float32)

        def receive(k, carry):
            z = lax.rem(place + k, group)
            if wait_slabs:
                pltpu.make_async_copy(slabs.at[z], slabs.at[z], slab_recv.at[z]).wait()

            def add(w, sums):
                kern_real = slabs[z, w, 0].astype(jnp.float32)
                kern_imag = slabs[z, w, 1].astype(jnp.float32)
                spec_real = spectra[w, :, :period]
                spec_imag = spectra[w, :, period:]
                return (
                    sums[0] + (kern_real * spec_real - kern_imag * spec_imag),
                    sums[1] + (kern_real * spec_imag + kern_imag * spec_real),
                )

            real, imag = lax.fori_loop(0, depths, add, (zero, zero), unroll=8)
            scattered[z, :, :period] = real
            scattered[z, :, period:] = imag
            return carry

        lax.fori_loop(0, group, receive, 0)

    def scatter(iteration, slot, s):
        pltpu.make_async_copy(in_a.at[slot, s], in_a.at[slot, s], recv_a.at[slot, s]).wait()
        blocks = [
            in_a[slot, s, :, l].astype(jnp.float32).reshape(depths * half, 2 * lanes)
            for l in range(lats)
        ]
        for h in range(2):
            along_y = jnp.concatenate(
                [b[:, h * lanes:(h + 1) * lanes] for b in blocks], axis=1
            ).astype(jnp.bfloat16)
            spectra[:, h * half:(h + 1) * half] = jnp.dot(
                along_y, forward_x[...], preferred_element_type=jnp.float32
            ).reshape(depths, half, 2 * period)
        couple(s, iteration == 0 and s == 0)
        along_x = jnp.dot(
            scattered[...].reshape(group * rows, 2 * period).astype(jnp.bfloat16),
            inverse_x[...],
            preferred_element_type=jnp.float32,
        )
        if iteration > 0:
            sent_b(s)
        for l in range(lats):
            mine = along_x[:, l * lanes:(l + 1) * lanes].reshape(group, 2, half, lanes)
            out_b[s, :, l] = jnp.concatenate([mine[:, 0], mine[:, 1]], axis=-1).astype(jnp.bfloat16)

    def gather_field(s):
        pltpu.make_async_copy(in_b.at[s], in_b.at[s], recv_b.at[s]).wait()
        blocks = in_b[s].astype(jnp.float32)
        along_x = jnp.stack(
            [blocks[:, :, :lanes], blocks[:, :, lanes:]], axis=1
        ).reshape(period, lanes).astype(jnp.bfloat16)
        turned = lax.dot_general(
            along_x, waves_y[...], (((0,), (0,)), ((), ())), preferred_element_type=jnp.float32
        )
        cosine = turned[:, :length].reshape(2, part, length)
        sine = turned[:, length:].reshape(2, part, length)
        sums = jnp.concatenate([cosine[0:1] - sine[1:2], cosine[1:2] + sine[0:1]], axis=0)
        return incident[0, s] + sums * (1.0 / float(period * period))

    for iteration in range(ITERS):
        slot = iteration % 2
        for s in range(sources_count):
            if iteration == 0:
                if s == 0:
                    for copy in copies[:3]:
                        copy.wait()
                field = incident[0, s]
            else:
                field = gather_field(s)
                sent_a(s)
            spread_along_y(s, field)
            if iteration > 0:
                exchange_a(slot, s)
        if iteration == 0:
            pl.semaphore_wait(barrier, devices - 1)
            for s in range(sources_count):
                exchange_a(slot, s)

            def deal(k, carry):
                slab_copy(k).start()
                return carry

            lax.fori_loop(1, group, deal, 0)
            for copy in copies[3:]:
                copy.wait()
        for s in range(sources_count):
            scatter(iteration, slot, s)
            exchange_b(s)
    for s in range(sources_count):
        out[0, s] = gather_field(s)
        sent_a(s)
        sent_b(s)

    def sent(k, carry):
        slab_copy(k).wait_send()
        return carry

    lax.fori_loop(1, group, sent, 0)


def born(depths, lats, incident, contrast, kernel):
    sources_count, part, length = incident.shape[1], incident.shape[3], incident.shape[4]
    period = 2 * length
    group = math.gcd(GROUP, depths)
    rows = period // (group * lats)
    half = rows // 2
    lanes = 4 * part
    block = jnp.bfloat16
    waves_y, forward_x, inverse_x = tables(length, lats)
    held = (incident, contrast, waves_y, forward_x, inverse_x)
    anywhere = pl.BlockSpec(memory_space=pl.ANY)
    return pl.pallas_call(
        functools.partial(born_kernel, depths, lats, group),
        out_shape=pltpu.VMEM(incident.shape, jnp.float32),
        in_specs=[anywhere] * 6,
        out_specs=pl.BlockSpec(memory_space=pltpu.VMEM),
        scratch_shapes=[pltpu.VMEM(a.shape, a.dtype) for a in held] + [
            pltpu.VMEM((group, depths, 2, rows, period), block),
            pltpu.VMEM((sources_count, group * lats, half, lanes), block),
            pltpu.VMEM((2, sources_count, depths, lats, half, lanes), block),
            pltpu.VMEM((sources_count, group, lats, half, lanes), block),
            pltpu.VMEM((sources_count, group * lats, half, lanes), block),
            pltpu.VMEM((depths, rows, 2 * period), jnp.float32),
            pltpu.VMEM((group, rows, 2 * period), jnp.float32),
            pltpu.SemaphoreType.DMA((len(held),)),
            pltpu.SemaphoreType.DMA((group,)),
            pltpu.SemaphoreType.DMA((group,)),
            pltpu.SemaphoreType.DMA((sources_count,)),
            pltpu.SemaphoreType.DMA((2, sources_count)),
            pltpu.SemaphoreType.DMA((sources_count,)),
            pltpu.SemaphoreType.DMA((sources_count,)),
        ],
        compiler_params=pltpu.CompilerParams(collective_id=0, has_side_effects=True),
        name="born",
    )(incident, contrast, kernel, waves_y, forward_x, inverse_x)


def solution(mesh):
    in_specs = (
        P("depth", None, None, "lat", None),
        P("depth", "lat", None),
        P("depth", None, None, "lat", None),
    )
    out_specs = P("depth", None, None, "lat", None)
    run = functools.partial(born, mesh.shape["depth"], mesh.shape["lat"])
    return jax.shard_map(run, mesh=mesh, in_specs=in_specs, out_specs=out_specs, check_vma=False)
```

time: 46.5 us -> 42.4 us (0.912)
  Pallas kernels: 44.8 us -> 41.5 us
  local copies, waits for them, and re-layouts: 1.47 us -> 0.63 us
    pallas_call x1, Pallas kernels: 44.8 us -> 41.5 us  [born(): pl.pallas_call(functools.partial(born_kernel, depths, lats, group), out_s...]
    unnamed x1, local copies, waits for them, and re-layouts: 1.47 us -> 0.63 us
where the time goes in v3:
time: 42.4 us; the launch traced here: 42.1 us
  Pallas kernels  41.5 us (98%)
  local copies, waits for them, and re-layouts  0.63 us (1%)
    pallas_call x1, Pallas kernels, born(): pl.pallas_call(functools.partial(born_kernel, depths, lats, group), out_s...  41.5 us

profile of v3, /device:TPU:0, one launch (start us, length us, event | category | flops | bytes accessed | tf_op | source)
XLA Modules:
  0.0 42.1 jit_solution(13290650537371040547)
XLA Ops:
  0.0 41.5 %born.1 = f32[1,2,2,32,128]{4,3,2,1,0:T(8,128)S(1)} custom-call(f32[1,2,2,32,128]{4,3,2,1,0:T(8,128)} %incident_hbm.1, f32[1,32,128]{2,1,0:T(8,128)} %contrast_hbm.1, bf16[1,8,2,64,256]{4,3,2,1,0:T(8,128)(2,1)} %green.1, bf16[256,256]{1,0:T(8,128)(2,1)} %constant.6.clone.waves_y_hbm, bf16[256,512]{1,0:T(8,128)(2,1)} %constant.7.clone.forward_x_hbm, ...), custom_call_target="tpu_custom_call" | custom-call | tf_op jit(solution)/shard_map/born/pallas_call | solution.py:268
  41.5 0.6 %copy.8 = f32[1,2,2,32,128]{4,3,2,1,0:T(8,128)} copy(f32[1,2,2,32,128]{4,3,2,1,0:T(8,128)S(1)} %born.1) | data formatting | bytes 131072

commit v4 on v3

--- a/solution.py
+++ b/solution.py
@@ -229,14 +229,15 @@
                 exchange_a(slot, s)
         if iteration == 0:
             pl.semaphore_wait(barrier, devices - 1)
-            for s in range(sources_count):
-                exchange_a(slot, s)
-
             def deal(k, carry):
                 slab_copy(k).start()
                 return carry
 
-            lax.fori_loop(1, group, deal, 0)
+            for s in range(sources_count):
+                exchange_a(slot, s)
+                if s == 0:
+                    lax.fori_loop(1, group, deal, 0)
+
             for copy in copies[3:]:
                 copy.wait()
         for s in range(sources_count):

time: 42.4 us -> 41.6 us (0.981)
  Pallas kernels: 41.5 us -> 40.8 us
    pallas_call x1, Pallas kernels: 41.5 us -> 40.8 us  [born(): pl.pallas_call(functools.partial(born_kernel, depths, lats, group), out_s...]
where the time goes in v4:
time: 41.6 us; the launch traced here: 41.4 us
  Pallas kernels  40.8 us (98%)
  local copies, waits for them, and re-layouts  0.63 us (2%)
    pallas_call x1, Pallas kernels, born(): pl.pallas_call(functools.partial(born_kernel, depths, lats, group), out_s...  40.8 us

profile of v4, /device:TPU:0, one launch (start us, length us, event | category | flops | bytes accessed | tf_op | source)
XLA Modules:
  0.0 41.4 jit_solution(18353006244635601070)
XLA Ops:
  0.0 40.8 %born.1 = f32[1,2,2,32,128]{4,3,2,1,0:T(8,128)S(1)} custom-call(f32[1,2,2,32,128]{4,3,2,1,0:T(8,128)} %incident_hbm.1, f32[1,32,128]{2,1,0:T(8,128)} %contrast_hbm.1, bf16[1,8,2,64,256]{4,3,2,1,0:T(8,128)(2,1)} %green.1, bf16[256,256]{1,0:T(8,128)(2,1)} %constant.6.clone.waves_y_hbm, bf16[256,512]{1,0:T(8,128)(2,1)} %constant.7.clone.forward_x_hbm, ...), custom_call_target="tpu_custom_call" | custom-call | tf_op jit(solution)/shard_map/born/pallas_call | solution.py:269
  40.8 0.6 %copy.8 = f32[1,2,2,32,128]{4,3,2,1,0:T(8,128)} copy(f32[1,2,2,32,128]{4,3,2,1,0:T(8,128)S(1)} %born.1) | data formatting | bytes 131072

commit v5 on v4

--- a/solution.py
+++ b/solution.py
@@ -149,7 +149,7 @@
             device_id=(first + d, lat), device_id_type=MESH,
         )
 
-    def couple(s, wait_slabs):
+    def couple(chains, wait_slabs):
         zero = jnp.zeros((rows, period), jnp.float32)
 
         def receive(k, carry):
@@ -157,24 +157,25 @@
             if wait_slabs:
                 pltpu.make_async_copy(slabs.at[z], slabs.at[z], slab_recv.at[z]).wait()
 
-            def add(w, sums):
+            def add(s, w, sums):
                 kern_real = slabs[z, w, 0].astype(jnp.float32)
                 kern_imag = slabs[z, w, 1].astype(jnp.float32)
-                spec_real = spectra[w, :, :period]
-                spec_imag = spectra[w, :, period:]
+                spec_real = spectra[s, w, :, :period]
+                spec_imag = spectra[s, w, :, period:]
                 return (
                     sums[0] + (kern_real * spec_real - kern_imag * spec_imag),
                     sums[1] + (kern_real * spec_imag + kern_imag * spec_real),
                 )
 
-            real, imag = lax.fori_loop(0, depths, add, (zero, zero), unroll=8)
-            scattered[z, :, :period] = real
-            scattered[z, :, period:] = imag
+            for s in chains:
+                real, imag = lax.fori_loop(0, depths, functools.partial(add, s), (zero, zero), unroll=8)
+                scattered[s, z, :, :period] = real
+                scattered[s, z, :, period:] = imag
             return carry
 
         lax.fori_loop(0, group, receive, 0)
 
-    def scatter(iteration, slot, s):
+    def spread_along_x(slot, s):
         pltpu.make_async_copy(in_a.at[slot, s], in_a.at[slot, s], recv_a.at[slot, s]).wait()
         blocks = [
             in_a[slot, s, :, l].astype(jnp.float32).reshape(depths * half, 2 * lanes)
@@ -184,12 +185,13 @@
             along_y = jnp.concatenate(
                 [b[:, h * lanes:(h + 1) * lanes] for b in blocks], axis=1
             ).astype(jnp.bfloat16)
-            spectra[:, h * half:(h + 1) * half] = jnp.dot(
+            spectra[s, :, h * half:(h + 1) * half] = jnp.dot(
                 along_y, forward_x[...], preferred_element_type=jnp.float32
             ).reshape(depths, half, 2 * period)
-        couple(s, iteration == 0 and s == 0)
+
+    def gather_along_x(iteration, s):
         along_x = jnp.dot(
-            scattered[...].reshape(group * rows, 2 * period).astype(jnp.bfloat16),
+            scattered[s].reshape(group * rows, 2 * period).astype(jnp.bfloat16),
             inverse_x[...],
             preferred_element_type=jnp.float32,
         )
@@ -240,8 +242,15 @@
 
             for copy in copies[3:]:
                 copy.wait()
+        if iteration == 0:
+            for s in range(sources_count):
+                spread_along_x(slot, s)
+            couple(range(sources_count), True)
         for s in range(sources_count):
-            scatter(iteration, slot, s)
+            if iteration > 0:
+                spread_along_x(slot, s)
+                couple((s,), False)
+            gather_along_x(iteration, s)
             exchange_b(s)
     for s in range(sources_count):
         out[0, s] = gather_field(s)
@@ -277,8 +286,8 @@
             pltpu.VMEM((2, sources_count, depths, lats, half, lanes), block),
             pltpu.VMEM((sources_count, group, lats, half, lanes), block),
             pltpu.VMEM((sources_count, group * lats, half, lanes), block),
-            pltpu.VMEM((depths, rows, 2 * period), jnp.float32),
-            pltpu.VMEM((group, rows, 2 * period), jnp.float32),
+            pltpu.VMEM((sources_count, depths, rows, 2 * period), jnp.float32),
+            pltpu.VMEM((sources_count, group, rows, 2 * period), jnp.float32),
             pltpu.SemaphoreType.DMA((len(held),)),
             pltpu.SemaphoreType.DMA((group,)),
             pltpu.SemaphoreType.DMA((group,)),

time: 41.6 us -> 43.7 us (1.050)
  Pallas kernels: 40.8 us -> 42.8 us
    pallas_call x1, Pallas kernels: 40.8 us -> 42.8 us  [born(): pl.pallas_call(functools.partial(born_kernel, depths, lats, group), out_s...]
where the time goes in v5:
time: 43.7 us; the launch traced here: 43.5 us
  Pallas kernels  42.8 us (98%)
  local copies, waits for them, and re-layouts  0.63 us (1%)
    pallas_call x1, Pallas kernels, born(): pl.pallas_call(functools.partial(born_kernel, depths, lats, group), out_s...  42.8 us

profile of v5, /device:TPU:0, one launch (start us, length us, event | category | flops | bytes accessed | tf_op | source)
XLA Modules:
  0.0 43.5 jit_solution(10989411082863986319)
XLA Ops:
  0.0 42.8 %born.1 = f32[1,2,2,32,128]{4,3,2,1,0:T(8,128)S(1)} custom-call(f32[1,2,2,32,128]{4,3,2,1,0:T(8,128)} %incident_hbm.1, f32[1,32,128]{2,1,0:T(8,128)} %contrast_hbm.1, bf16[1,8,2,64,256]{4,3,2,1,0:T(8,128)(2,1)} %green.1, bf16[256,256]{1,0:T(8,128)(2,1)} %constant.6.clone.waves_y_hbm, bf16[256,512]{1,0:T(8,128)(2,1)} %constant.7.clone.forward_x_hbm, ...), custom_call_target="tpu_custom_call" | custom-call | tf_op jit(solution)/shard_map/born/pallas_call | solution.py:278
  42.9 0.6 %copy.8 = f32[1,2,2,32,128]{4,3,2,1,0:T(8,128)} copy(f32[1,2,2,32,128]{4,3,2,1,0:T(8,128)S(1)} %born.1) | data formatting | bytes 131072
